TPU v7x, 32 devices: a whole 2x2x4 slice. The times are simulated.
32 devices in a mesh: member: 2 (over x), row: 16 (over z, y, core).
Axes of the slice: x: 2, y: 2, z: 4, core: 2. Of those that a mesh axis runs over, the one named last changes fastest.
Arguments:
- innovation: bfloat16 [8, 1024, 2048], P('member', 'row'), parts along dimension 0, may hold values from -6 to 6
- background: bfloat16 [8, 1024, 2048], P('member', 'row'), parts along dimension 0, may hold values from -6 to 6
- level_weight: float32 [4], replicated, may hold values from 0.25 to 4
Outputs:
- displacement: float32 [4, 1024, 2048], P('member', 'row'), parts along dimension 0
There are 2 independent parts, one for each index of `member`. A program takes and returns all parts, laid end to end along the dimension named above; an argument that names none is the same for every part. Nothing has to cross between parts.
All inputs are finite; a program needn't handle non-finite values.
Results may differ from a plain program's by a relative error of at most 0.0003.
Values may be sent and summed in bfloat16 or wider, within the bound.
A program may use at most 64 MiB of HBM per device.

v0:
```python
import jax
import jax.numpy as jnp
from jax import lax
from jax.sharding import PartitionSpec as P

HALF = 64
SIGMA = 64


def padded_2(block, sides, width):
    for axis, dim in sides:
        count = lax.axis_size(axis)
        forward = [(i, i + 1) for i in range(count - 1)]
        backward = [(target, source) for source, target in forward]
        low = lax.ppermute(
            lax.slice_in_dim(block, block.shape[dim] - width, None, axis=dim), axis, forward
        )
        high = lax.ppermute(lax.slice_in_dim(block, 0, width, axis=dim), axis, backward)
        block = jnp.concatenate([low, block, high], axis=dim)
    return block


def tap_at(offset):
    grid = jnp.arange(-HALF, HALF + 1).astype(jnp.float32)
    spread = jnp.float32(SIGMA)
    total = jnp.sqrt(jnp.sum(jnp.exp(-grid * grid / (spread * spread))))
    off = offset.astype(jnp.float32)
    value = jnp.exp(-off * off / (2.0 * spread * spread)) / total
    return jnp.where(jnp.abs(offset) <= HALF, value, jnp.float32(0.0))


def band_blocks():
    inner = jnp.arange(128)[:, None]
    outer = jnp.arange(128)[None, :]
    return [tap_at(128 * shift + inner - outer) for shift in (-1, 0, 1)]


def smooth_last(values, blocks):
    lead = values.shape[:-1]
    length = values.shape[-1]
    nblocks = length // 128
    widths = [(0, 0)] * (values.ndim - 1) + [(128, 128)]
    padded = jnp.pad(values, widths).reshape(lead + (nblocks + 2, 128))
    total = jnp.zeros(lead + (nblocks, 128), jnp.float32)
    for index in range(3):
        part = padded[..., index : index + nblocks, :]
        total = total + jnp.dot(
            part, blocks[index], precision=lax.Precision.HIGHEST, preferred_element_type=jnp.float32
        )
    return total.reshape(lead + (length,))


def smooth_mid(values, blocks):
    chans, length, width = values.shape
    nblocks = length // 128
    padded = jnp.pad(values, ((0, 0), (128, 128), (0, 0))).reshape(chans, nblocks + 2, 128, width)
    total = jnp.zeros((chans, nblocks, 128, width), jnp.float32)
    for index in range(3):
        part = padded[:, index : index + nblocks]
        total = total + jnp.einsum(
            "cbix,io->cbox",
            part,
            blocks[index],
            precision=lax.Precision.HIGHEST,
            preferred_element_type=jnp.float32,
        )
    return total.reshape(chans, length, width)


def body(innovation, background, level_weight):
    blocks = band_blocks()
    rimmed = padded_2(background, (("row", 1),), 1).astype(jnp.float32)
    grad_y = 0.5 * (rimmed[:, 2:, :] - rimmed[:, :-2, :])
    padded_x = jnp.pad(rimmed[:, 1:-1, :], ((0, 0), (0, 0), (1, 1)))
    grad_x = 0.5 * (padded_x[:, :, 2:] - padded_x[:, :, :-2])
    scaled = level_weight[:, None, None] * innovation.astype(jnp.float32)
    numer_y = jnp.sum(scaled * grad_y, axis=0)
    numer_x = jnp.sum(scaled * grad_x, axis=0)
    denom = 1.0 + jnp.sum(level_weight[:, None, None] * (grad_y * grad_y + grad_x * grad_x), axis=0)
    raw = jnp.stack([numer_y / denom, numer_x / denom])
    zonal = smooth_last(raw, blocks)
    smoothed = smooth_mid(
        lax.all_to_all(zonal, "row", split_axis=2, concat_axis=1, tiled=True), blocks
    )
    return lax.all_to_all(smoothed, "row", split_axis=1, concat_axis=2, tiled=True)


def solution(mesh):
    placed = (P("member", "row", None), P("member", "row", None), P())
    return jax.shard_map(
        body, mesh=mesh, in_specs=placed, out_specs=P("member", "row", None), check_vma=False
    )
```

profile of v0, /device:TPU:1, one launch (start us, length us, event | category | flops | bytes accessed | tf_op | source)
XLA Modules:
  0.0 95.4 jit_solution(1240667817818672247)
XLA Ops:
  0.0 1.0 %fusion.82 = (bf16[4,1,2048]{2,1,0:T(2,128)(2,1)S(1)}, bf16[4,1,2048]{2,1,0:T(2,128)(2,1)S(1)}) fusion(bf16[4,64,2048]{2,1,0:T(8,128)(2,1)} %param.4), kind=kLoop, calls=%fused_computation.102 | loop fusion | bytes 65536 | tf_op jit(solution)/shard_map/slice | solution.py:16
  1.0 4.5 %collective-permute-start = (bf16[4,1,2048]{2,1,0:T(2,128)(2,1)S(1)}, bf16[4,1,2048]{2,1,0:T(2,128)(2,1)S(1)}, u32[]{:S(2)}, u32[]{:S(2)}) collective-permute-start(bf16[4,1,2048]{2,1,0:T(2,128)(2,1)S(1)} %get-tuple-element.8), channel_id=1, source_target_pairs={{0,1},{1,2},{2,3},{3,4},{4,5},{5,6},{6,7},{7,8},{8,9},{9,10},{10,1... | collective-permute-start | bytes 49160 | tf_op jit(solution)/shard_map/ppermute | solution.py:15
  5.6 1.9 %collective-permute-start.1 = (bf16[4,1,2048]{2,1,0:T(2,128)(2,1)S(1)}, bf16[4,1,2048]{2,1,0:T(2,128)(2,1)S(1)}, u32[]{:S(2)}, u32[]{:S(2)}) collective-permute-start(bf16[4,1,2048]{2,1,0:T(2,128)(2,1)S(1)} %get-tuple-element.9), channel_id=1, source_target_pairs={{1,0},{2,1},{3,2},{4,3},{5,4},{6,5},{7,6},{8,7},{9,8},{10,9},{11,1... | collective-permute-start | bytes 49160 | tf_op jit(solution)/shard_map/ppermute | solution.py:18
  7.5 0.6 fusion.63
  8.8 0.0 collective-permute-done
  8.8 2.0 %collective-permute-done.1 = bf16[4,1,2048]{2,1,0:T(2,128)(2,1)S(1)} collective-permute-done((bf16[4,1,2048]{2,1,0:T(2,128)(2,1)S(1)}, bf16[4,1,2048]{2,1,0:T(2,128)(2,1)S(1)}, u32[]{:S(2)}, u32[]{:S(2)}) %collective-permute-start.1) | collective-permute-done | bytes 16416 | tf_op jit(solution)/shard_map/ppermute | solution.py:18
  10.8 1.6 %maximum_convert_fusion = f32[4,66,2048]{2,1,0:T(8,128)S(1)} fusion(bf16[4,1,2048]{2,1,0:T(2,128)(2,1)S(1)} %collective-permute-done.1, bf16[4,64,2048]{2,1,0:T(8,128)(2,1)} %param.4, bf16[4,1,2048]{2,1,0:T(2,128)(2,1)S(1)} %collective-permute-done), kind=kLoop, calls=%fused_computation.17 | loop fusion | flops 3244032 | bytes 3244032 | tf_op jit(solution)/shard_map/convert_element_type | solution.py:72
  12.4 0.0 copy-start
  12.4 0.0 copy-start.1
  12.4 0.3 slice.54
  12.7 0.9 copy-done
  13.6 0.0 copy-done.1
  13.6 2.7 %multiply_reduce_fusion.2 = (f32[64,2048]{1,0:T(8,128)S(1)}, f32[64,2048]{1,0:T(8,128)S(1)}, f32[64,2048]{1,0:T(8,128)S(1)}) fusion(bf16[4,64,2048]{2,1,0:T(8,128)(2,1)S(1)} %copy-done, f32[4]{0:T(128)S(1)} %copy-done.1, f32[4,66,2048]{2,1,0:T(8,128)S(1)} %maximum_convert_fusion, f32[4,64,2048]{2,1,0:T(8,128)S(1)} %slice.54), kind=kLoop, calls=%fused_computation.8 | loop fusion | flops 8519680 | bytes 8912912 | tf_op jit(solution)/shard_map/reduce_sum | solution.py:77
  16.3 0.1 divide_bitcast_fusion.1
  16.4 0.1 select_maximum_fusion
  16.5 0.2 reshape.52
  16.7 1.0 %fusion.10 = f32[2,64,16,128]{3,2,1,0:T(8,128)S(1)} fusion(f32[2,64,18,128]{3,2,1,0:T(8,128)S(1)} %reshape.52, f32[]{:T(128)S(6)} %sqrt.2, s32[128]{0:T(128)S(1)} %iota_add_fusion.1), kind=kOutput, calls=%fused_computation.25 | convolution fusion | flops 402800640 | bytes 2097668 | tf_op jit(solution)/shard_map/dot_general | solution.py:47
  17.7 1.0 %convolution_add_fusion.3 = f32[2,64,16,128]{3,2,1,0:T(8,128)S(1)} fusion(f32[2,64,16,128]{3,2,1,0:T(8,128)S(1)} %fusion.10, f32[2,64,18,128]{3,2,1,0:T(8,128)S(1)} %reshape.52, f32[]{:T(128)S(6)} %sqrt.2), kind=kOutput, calls=%fused_computation.15 | convolution fusion | flops 403062784 | bytes 3145732 | tf_op jit(solution)/shard_map/dot_general | solution.py:47
  18.7 1.0 %convolution_add_fusion.2 = f32[2,64,16,128]{3,2,1,0:T(8,128)S(1)} fusion(f32[2,64,16,128]{3,2,1,0:T(8,128)S(1)} %convolution_add_fusion.3, f32[2,64,18,128]{3,2,1,0:T(8,128)S(1)} %reshape.52, s32[128]{0:T(128)S(1)} %iota_add_fusion, f32[]{:T(128)S(6)} %sqrt.2), kind=kOutput, calls=%fused_computation.14 | convolution fusion | flops 403062784 | bytes 3146244 | tf_op jit(solution)/shard_map/dot_general | solution.py:47
  19.7 1.0 %copy.30 = f32[2,64,16,128]{1,0,3,2:T(2,128)S(1)} copy(f32[2,64,16,128]{3,2,1,0:T(8,128)S(1)} %convolution_add_fusion.2) | data formatting | bytes 2097152 | tf_op jit(solution)/shard_map/reshape | solution.py:50
  20.8 2.2 %reshape.62 = f32[16,1,16384]{2,1,0:T(1,128)S(1)} reshape(f32[2048,2,64]{2,1,0:T(2,128)S(1)} %bitcast.44) | data formatting | bytes 2097152
  23.0 30.9 %all_to_all.36 = f32[16,1,16384]{2,1,0:T(1,128)S(1)} all-to-all(f32[16,1,16384]{2,1,0:T(1,128)S(1)} %reshape.62), channel_id=1, replica_groups=mesh['member'=2,'row'=16] {'row'}, dimensions={0} | all-to-all | bytes 2097152 | tf_op jit(solution)/shard_map/all_to_all | solution.py:83
  53.8 0.5 broadcast.123
  54.3 3.1 %reduce = f32[16,16384]{1,0:T(8,128)S(1)} reduce(f32[16,1,16384]{2,1,0:T(1,128)S(1)} %all_to_all.36, f32[]{:T(128)} %broadcast.123), dimensions={1}, to_apply=%all_to_all.26.reduce_sub_computation | reduce | bytes 2097156 | tf_op jit(solution)/shard_map/all_to_all | solution.py:83
  57.5 1.5 %reshape.63 = f32[2048,2,64]{2,1,0:T(2,128)S(1)} reshape(f32[16,16384]{1,0:T(8,128)S(1)} %reduce) | data formatting | bytes 2097152
  59.0 0.9 copy.18
  60.0 0.1 pad.14
  60.1 1.1 %fusion.6 = f32[128,2,8,128]{3,0,2,1:T(8,128)S(1)} fusion(f32[2,10,128,128]{3,2,1,0:T(8,128)S(1)} %bitcast.41, f32[]{:T(128)S(6)} %sqrt.2, s32[128]{0:T(128)S(1)} %iota_add_fusion.1), kind=kOutput, calls=%fused_computation.21 | convolution fusion | flops 402800640 | bytes 2097668 | tf_op jit(solution)/shard_map/cbix,io->cbox/dot_general | solution.py:60
  61.1 1.1 %convolution_add_fusion.1 = f32[128,2,8,128]{3,0,2,1:T(8,128)S(1)} fusion(f32[128,2,8,128]{3,0,2,1:T(8,128)S(1)} %fusion.6, f32[2,10,128,128]{3,2,1,0:T(8,128)S(1)} %bitcast.42, f32[]{:T(128)S(6)} %sqrt.2), kind=kOutput, calls=%fused_computation.13 | convolution fusion | flops 403062784 | bytes 3145732 | tf_op jit(solution)/shard_map/cbix,io->cbox/dot_general | solution.py:60
  62.2 1.1 %convolution_add_fusion = f32[128,2,8,128]{3,0,2,1:T(8,128)S(1)} fusion(f32[128,2,8,128]{3,0,2,1:T(8,128)S(1)} %convolution_add_fusion.1, f32[2,10,128,128]{3,2,1,0:T(8,128)S(1)} %bitcast.43, s32[128]{0:T(128)S(1)} %iota_add_fusion, f32[]{:T(128)S(6)} %sqrt.2), kind=kOutput, calls=%fused_computation.12 | convolution fusion | flops 403062784 | bytes 3146244 | tf_op jit(solution)/shard_map/cbix,io->cbox/dot_general | solution.py:60
  63.3 0.8 copy.19
  64.1 29.5 %all_to_all.37 = f32[2,1024,128]{2,0,1:T(2,128)S(1)} all-to-all(f32[2,1024,128]{2,0,1:T(2,128)S(1)} %copy.19), channel_id=1, replica_groups=mesh['member'=2,'row'=16] {'row'}, dimensions={1} | all-to-all | bytes 2097152 | tf_op jit(solution)/shard_map/all_to_all | solution.py:85
  93.6 0.6 copy.20
  94.2 1.1 %all_to_all.33 = f32[2,64,2048]{2,1,0:T(8,128)} reshape(f32[2,64,16,128]{3,2,1,0:T(8,128)S(1)} %copy.20) | data formatting | bytes 2097152 | tf_op jit(solution)/shard_map/all_to_all | solution.py:85
  (2 shorter events, 0.0 us)
Async XLA Ops:
  1.0 7.8 %collective-permute-start = (bf16[4,1,2048]{2,1,0:T(2,128)(2,1)S(1)}, bf16[4,1,2048]{2,1,0:T(2,128)(2,1)S(1)}, u32[]{:S(2)}, u32[]{:S(2)}) collective-permute-start(bf16[4,1,2048]{2,1,0:T(2,128)(2,1)S(1)} %get-tuple-element.8), channel_id=1, source_target_pairs={{0,1},{1,2},{2,3},{3,4},{4,5},{5,6},{6,7},{7,8},{8,9},{9,10},{10,1... | collective-permute-start | bytes 49160 | tf_op jit(solution)/shard_map/ppermute | solution.py:15
  5.6 5.2 %collective-permute-start.1 = (bf16[4,1,2048]{2,1,0:T(2,128)(2,1)S(1)}, bf16[4,1,2048]{2,1,0:T(2,128)(2,1)S(1)}, u32[]{:S(2)}, u32[]{:S(2)}) collective-permute-start(bf16[4,1,2048]{2,1,0:T(2,128)(2,1)S(1)} %get-tuple-element.9), channel_id=1, source_target_pairs={{1,0},{2,1},{3,2},{4,3},{5,4},{6,5},{7,6},{8,7},{9,8},{10,9},{11,1... | collective-permute-start | bytes 49160 | tf_op jit(solution)/shard_map/ppermute | solution.py:18
  12.4 1.2 %copy-start = (bf16[4,64,2048]{2,1,0:T(8,128)(2,1)S(1)}, bf16[4,64,2048]{2,1,0:T(8,128)(2,1)}, u32[]{:S(2)}) copy-start(bf16[4,64,2048]{2,1,0:T(8,128)(2,1)} %param.3) | copy-start | bytes 3145732
  12.4 1.2 %copy-start.1 = (f32[4]{0:T(128)S(1)}, f32[4]{0:T(128)}, u32[]{:S(2)}) copy-start(f32[4]{0:T(128)} %param.5) | copy-start | bytes 52
where the time goes:
time: 95.7 us; the launch traced here: 95.4 us
  blocking collectives  60.4 us (63%)
  local copies, waits for them, and re-layouts  11.2 us (12%)
  other arithmetic  8.24 us (9%)
  starting transfers between devices  6.45 us (7%)
  matrix products  6.23 us (7%)
  waiting for transfers between devices  1.97 us (2%)
    all_to_all x1, blocking collectives, body(): lax.all_to_all(zonal, 'row', split_axis=2, concat_axis=1, tiled=True)  30.9 us
    all_to_all x1, blocking collectives, body(): lax.all_to_all(smoothed, 'row', split_axis=1, concat_axis=2, tiled=True)  29.5 us
    unnamed x6, local copies, waits for them, and re-layouts  4.65 us
    ppermute x1, starting transfers between devices, padded_2(): lax.ppermute(lax.slice_in_dim(block, block.shape[dim] - width, None, axis...  4.53 us
    dot_general x3, matrix products, smooth_mid(): jnp.einsum('cbix,io->cbox', part, blocks[index], precision=lax.Precision....  3.21 us
    all_to_all x1, other arithmetic, body(): lax.all_to_all(zonal, 'row', split_axis=2, concat_axis=1, tiled=True)  3.15 us
    dot_general x3, matrix products, smooth_last(): jnp.dot(part, blocks[index], precision=lax.Precision.HIGHEST, preferred_e...  3.02 us
    reduce_sum x1, other arithmetic, body(): numer_y = jnp.sum(scaled * grad_y, axis=0)  2.69 us
  transfers between devices with their start and end apart: 2, of which 1 were waited for; matrix products, arithmetic and copies ran while one was open for 1% of the time, Pallas kernels for 0%

commit v1 on v0

--- a/solution.py
+++ b/solution.py
@@ -80,7 +80,11 @@
     raw = jnp.stack([numer_y / denom, numer_x / denom])
     zonal = smooth_last(raw, blocks)
     smoothed = smooth_mid(
-        lax.all_to_all(zonal, "row", split_axis=2, concat_axis=1, tiled=True), blocks
+        jnp.concatenate(
+            lax.all_to_all(jnp.stack(jnp.split(zonal, lax.axis_size("row"), axis=2)), "row", 0, 0),
+            axis=1,
+        ),
+        blocks,
     )
     return lax.all_to_all(smoothed, "row", split_axis=1, concat_axis=2, tiled=True)
 

time: 95.7 us -> 86.9 us (0.908)
  local copies, waits for them, and re-layouts: 11.2 us -> 5.44 us
  other arithmetic: 8.24 us -> 5.09 us
    unnamed x6 -> x19, local copies, waits for them, and re-layouts: 4.65 us -> 1.11 us
    all_to_all x1 -> x0, other arithmetic: 3.15 us -> none  [body(): lax.all_to_all(zonal, 'row', split_axis=2, concat_axis=1, tiled=True)]
    all_to_all x2 -> x1, local copies, waits for them, and re-layouts: 1.44 us -> 0.07 us  [body(): lax.all_to_all(jnp.stack(jnp.split(zonal, lax.axis_size('row'), axis=2)),...]
where the time goes in v1:
time: 86.9 us; the launch traced here: 86.6 us
  blocking collectives  60.4 us (70%)
  starting transfers between devices  6.45 us (7%)
  matrix products  6.22 us (7%)
  local copies, waits for them, and re-layouts  5.44 us (6%)
  other arithmetic  5.09 us (6%)
  waiting for transfers between devices  1.97 us (2%)
  between operations  1 us (1%)
    all_to_all x1, blocking collectives, body(): lax.all_to_all(jnp.stack(jnp.split(zonal, lax.axis_size('row'), axis=2)),...  30.9 us
    all_to_all x1, blocking collectives, body(): lax.all_to_all(smoothed, 'row', split_axis=1, concat_axis=2, tiled=True)  29.5 us
    ppermute x1, starting transfers between devices, padded_2(): lax.ppermute(lax.slice_in_dim(block, block.shape[dim] - width, None, axis...  4.53 us
    dot_general x3, matrix products, smooth_mid(): jnp.einsum('cbix,io->cbox', part, blocks[index], precision=lax.Precision....  3.21 us
    dot_general x3, matrix products, smooth_last(): jnp.dot(part, blocks[index], precision=lax.Precision.HIGHEST, preferred_e...  3.01 us
    reduce_sum x1, other arithmetic, body(): numer_y = jnp.sum(scaled * grad_y, axis=0)  2.69 us
    ppermute x1, waiting for transfers between devices, padded_2(): lax.ppermute(lax.slice_in_dim(block, 0, width, axis=dim), axis, backward)  1.96 us
    ppermute x1, starting transfers between devices, padded_2(): lax.ppermute(lax.slice_in_dim(block, 0, width, axis=dim), axis, backward)  1.92 us
  transfers between devices with their start and end apart: 2, of which 1 were waited for; matrix products, arithmetic and copies ran while one was open for 1% of the time, Pallas kernels for 0%

profile of v1, /device:TPU:1, one launch (start us, length us, event | category | flops | bytes accessed | tf_op | source)
XLA Modules:
  0.0 86.6 jit_solution(18088368372990632270)
XLA Ops:
  0.0 1.0 %fusion.98 = (bf16[4,1,2048]{2,1,0:T(2,128)(2,1)S(1)}, bf16[4,1,2048]{2,1,0:T(2,128)(2,1)S(1)}) fusion(bf16[4,64,2048]{2,1,0:T(8,128)(2,1)} %param.4), kind=kLoop, calls=%fused_computation.134 | loop fusion | bytes 65536 | tf_op jit(solution)/shard_map/slice | solution.py:16
  1.0 4.5 %collective-permute-start = (bf16[4,1,2048]{2,1,0:T(2,128)(2,1)S(1)}, bf16[4,1,2048]{2,1,0:T(2,128)(2,1)S(1)}, u32[]{:S(2)}, u32[]{:S(2)}) collective-permute-start(bf16[4,1,2048]{2,1,0:T(2,128)(2,1)S(1)} %get-tuple-element.8), channel_id=1, source_target_pairs={{0,1},{1,2},{2,3},{3,4},{4,5},{5,6},{6,7},{7,8},{8,9},{9,10},{10,1... | collective-permute-start | bytes 49160 | tf_op jit(solution)/shard_map/ppermute | solution.py:15
  5.6 1.9 %collective-permute-start.1 = (bf16[4,1,2048]{2,1,0:T(2,128)(2,1)S(1)}, bf16[4,1,2048]{2,1,0:T(2,128)(2,1)S(1)}, u32[]{:S(2)}, u32[]{:S(2)}) collective-permute-start(bf16[4,1,2048]{2,1,0:T(2,128)(2,1)S(1)} %get-tuple-element.9), channel_id=1, source_target_pairs={{1,0},{2,1},{3,2},{4,3},{5,4},{6,5},{7,6},{8,7},{9,8},{10,9},{11,1... | collective-permute-start | bytes 49160 | tf_op jit(solution)/shard_map/ppermute | solution.py:18
  7.5 0.6 fusion.79
  8.8 0.0 collective-permute-done
  8.8 2.0 %collective-permute-done.1 = bf16[4,1,2048]{2,1,0:T(2,128)(2,1)S(1)} collective-permute-done((bf16[4,1,2048]{2,1,0:T(2,128)(2,1)S(1)}, bf16[4,1,2048]{2,1,0:T(2,128)(2,1)S(1)}, u32[]{:S(2)}, u32[]{:S(2)}) %collective-permute-start.1) | collective-permute-done | bytes 16416 | tf_op jit(solution)/shard_map/ppermute | solution.py:18
  10.8 1.6 %maximum_convert_fusion = f32[4,66,2048]{2,1,0:T(8,128)S(1)} fusion(bf16[4,1,2048]{2,1,0:T(2,128)(2,1)S(1)} %collective-permute-done.1, bf16[4,64,2048]{2,1,0:T(8,128)(2,1)} %param.4, bf16[4,1,2048]{2,1,0:T(2,128)(2,1)S(1)} %collective-permute-done), kind=kLoop, calls=%fused_computation.17 | loop fusion | flops 3244032 | bytes 3244032 | tf_op jit(solution)/shard_map/convert_element_type | solution.py:72
  12.4 0.0 copy-start
  12.4 0.0 copy-start.1
  12.4 0.3 slice.54
  12.7 0.9 %copy-done = bf16[4,64,2048]{2,1,0:T(8,128)(2,1)S(1)} copy-done((bf16[4,64,2048]{2,1,0:T(8,128)(2,1)S(1)}, bf16[4,64,2048]{2,1,0:T(8,128)(2,1)}, u32[]{:S(2)}) %copy-start) | copy-done | bytes 1048600
  13.6 0.0 copy-done.1
  13.6 2.7 %multiply_reduce_fusion.2 = (f32[64,2048]{1,0:T(8,128)S(1)}, f32[64,2048]{1,0:T(8,128)S(1)}, f32[64,2048]{1,0:T(8,128)S(1)}) fusion(bf16[4,64,2048]{2,1,0:T(8,128)(2,1)S(1)} %copy-done, f32[4]{0:T(128)S(1)} %copy-done.1, f32[4,66,2048]{2,1,0:T(8,128)S(1)} %maximum_convert_fusion, f32[4,64,2048]{2,1,0:T(8,128)S(1)} %slice.54), kind=kLoop, calls=%fused_computation.8 | loop fusion | flops 8519680 | bytes 8912912 | tf_op jit(solution)/shard_map/reduce_sum | solution.py:77
  16.3 0.1 divide_bitcast_fusion.1
  16.4 0.1 select_maximum_fusion
  16.5 0.2 reshape.58
  16.7 1.0 %fusion.10 = f32[2,64,16,128]{3,2,1,0:T(8,128)S(1)} fusion(f32[2,64,18,128]{3,2,1,0:T(8,128)S(1)} %reshape.58, f32[]{:T(128)S(6)} %sqrt.2, s32[128]{0:T(128)S(1)} %iota_add_fusion.1), kind=kOutput, calls=%fused_computation.25 | convolution fusion | flops 402800640 | bytes 2097668 | tf_op jit(solution)/shard_map/dot_general | solution.py:47
  17.7 1.0 %convolution_add_fusion.3 = f32[2,64,16,128]{3,2,1,0:T(8,128)S(1)} fusion(f32[2,64,16,128]{3,2,1,0:T(8,128)S(1)} %fusion.10, f32[2,64,18,128]{3,2,1,0:T(8,128)S(1)} %reshape.58, f32[]{:T(128)S(6)} %sqrt.2), kind=kOutput, calls=%fused_computation.15 | convolution fusion | flops 403062784 | bytes 3145732 | tf_op jit(solution)/shard_map/dot_general | solution.py:47
  18.7 1.0 %convolution_add_fusion.2 = f32[2,64,16,128]{3,2,1,0:T(8,128)S(1)} fusion(f32[2,64,16,128]{3,2,1,0:T(8,128)S(1)} %convolution_add_fusion.3, f32[2,64,18,128]{3,2,1,0:T(8,128)S(1)} %reshape.58, s32[128]{0:T(128)S(1)} %iota_add_fusion, f32[]{:T(128)S(6)} %sqrt.2), kind=kOutput, calls=%fused_computation.14 | convolution fusion | flops 403062784 | bytes 3146244 | tf_op jit(solution)/shard_map/dot_general | solution.py:47
  19.7 0.2 reshape.59
  20.2 30.9 %all_to_all.23 = f32[16,2,64,128]{3,2,1,0:T(8,128)S(1)} all-to-all(f32[16,2,64,128]{3,2,1,0:T(8,128)S(1)} %fusion.27), channel_id=1, replica_groups=mesh['member'=2,'row'=16] {'row'}, dimensions={0} | all-to-all | bytes 2097152 | tf_op jit(solution)/shard_map/all_to_all | solution.py:84
  51.1 0.1 copy.30
  51.2 0.1 pad.14
  51.3 1.1 %fusion.6 = f32[128,2,8,128]{3,0,2,1:T(8,128)S(1)} fusion(f32[2,10,128,128]{3,2,1,0:T(8,128)S(1)} %bitcast.103, f32[]{:T(128)S(6)} %sqrt.2, s32[128]{0:T(128)S(1)} %iota_add_fusion.1), kind=kOutput, calls=%fused_computation.21 | convolution fusion | flops 402800640 | bytes 2097668 | tf_op jit(solution)/shard_map/cbix,io->cbox/dot_general | solution.py:60
  52.3 1.1 %convolution_add_fusion.1 = f32[128,2,8,128]{3,0,2,1:T(8,128)S(1)} fusion(f32[128,2,8,128]{3,0,2,1:T(8,128)S(1)} %fusion.6, f32[2,10,128,128]{3,2,1,0:T(8,128)S(1)} %bitcast.104, f32[]{:T(128)S(6)} %sqrt.2), kind=kOutput, calls=%fused_computation.13 | convolution fusion | flops 403062784 | bytes 3145732 | tf_op jit(solution)/shard_map/cbix,io->cbox/dot_general | solution.py:60
  53.4 1.1 %convolution_add_fusion = f32[128,2,8,128]{3,0,2,1:T(8,128)S(1)} fusion(f32[128,2,8,128]{3,0,2,1:T(8,128)S(1)} %convolution_add_fusion.1, f32[2,10,128,128]{3,2,1,0:T(8,128)S(1)} %bitcast.105, s32[128]{0:T(128)S(1)} %iota_add_fusion, f32[]{:T(128)S(6)} %sqrt.2), kind=kOutput, calls=%fused_computation.12 | convolution fusion | flops 403062784 | bytes 3146244 | tf_op jit(solution)/shard_map/cbix,io->cbox/dot_general | solution.py:60
  54.5 0.8 copy.31
  55.3 29.5 %all_to_all.24 = f32[2,1024,128]{2,0,1:T(2,128)S(1)} all-to-all(f32[2,1024,128]{2,0,1:T(2,128)S(1)} %copy.31), channel_id=1, replica_groups=mesh['member'=2,'row'=16] {'row'}, dimensions={1} | all-to-all | bytes 2097152 | tf_op jit(solution)/shard_map/all_to_all | solution.py:89
  84.8 0.6 copy.32
  85.4 1.1 %all_to_all.20 = f32[2,64,2048]{2,1,0:T(8,128)} reshape(f32[2,64,16,128]{3,2,1,0:T(8,128)S(1)} %copy.32) | data formatting | bytes 2097152 | tf_op jit(solution)/shard_map/all_to_all | solution.py:89
  (18 shorter events, 0.2 us)
Async XLA Ops:
  1.0 7.8 %collective-permute-start = (bf16[4,1,2048]{2,1,0:T(2,128)(2,1)S(1)}, bf16[4,1,2048]{2,1,0:T(2,128)(2,1)S(1)}, u32[]{:S(2)}, u32[]{:S(2)}) collective-permute-start(bf16[4,1,2048]{2,1,0:T(2,128)(2,1)S(1)} %get-tuple-element.8), channel_id=1, source_target_pairs={{0,1},{1,2},{2,3},{3,4},{4,5},{5,6},{6,7},{7,8},{8,9},{9,10},{10,1... | collective-permute-start | bytes 49160 | tf_op jit(solution)/shard_map/ppermute | solution.py:15
  5.6 5.2 %collective-permute-start.1 = (bf16[4,1,2048]{2,1,0:T(2,128)(2,1)S(1)}, bf16[4,1,2048]{2,1,0:T(2,128)(2,1)S(1)}, u32[]{:S(2)}, u32[]{:S(2)}) collective-permute-start(bf16[4,1,2048]{2,1,0:T(2,128)(2,1)S(1)} %get-tuple-element.9), channel_id=1, source_target_pairs={{1,0},{2,1},{3,2},{4,3},{5,4},{6,5},{7,6},{8,7},{9,8},{10,9},{11,1... | collective-permute-start | bytes 49160 | tf_op jit(solution)/shard_map/ppermute | solution.py:18
  12.4 1.2 %copy-start = (bf16[4,64,2048]{2,1,0:T(8,128)(2,1)S(1)}, bf16[4,64,2048]{2,1,0:T(8,128)(2,1)}, u32[]{:S(2)}) copy-start(bf16[4,64,2048]{2,1,0:T(8,128)(2,1)} %param.3) | copy-start | bytes 3145732
  12.4 1.2 %copy-start.1 = (f32[4]{0:T(128)S(1)}, f32[4]{0:T(128)}, u32[]{:S(2)}) copy-start(f32[4]{0:T(128)} %param.5) | copy-start | bytes 52
